TPU v7x, 32 devices: a whole 2x2x4 slice. The times are simulated.
32 devices in a mesh: wide: 8 (over y, x, core), narrow: 4 (over z).
Axes of the slice: x: 2, y: 2, z: 4, core: 2. Of those that a mesh axis runs over, the one named last changes fastest.
Arguments:
- hidden: bfloat16 [1024, 4096], P('wide', 'narrow'), may hold values from -6 to 6
- head_weight: bfloat16 [32768, 4096], P('wide', 'narrow'), may hold values from -0.25 to 0.25
- lse: float32 [1024], replicated, may hold values from 12 to 14
- targets: int32 [1024], replicated, may hold values from 0 to 32767
- loss_weight: float32 [1024], replicated, may hold values from 16 to 48
- block_tiles: int32 [8, 8, 4], P(None, 'wide'), may hold values from 0 to 31, as said below
- block_counts: int32 [8, 8], P(None, 'wide'), may hold values from 0 to 4, as said below
- gate_pre: bfloat16 [1024, 7168], P('wide', 'narrow'), may hold values from -6 to 6
- up_pre: bfloat16 [1024, 7168], P('wide', 'narrow'), may hold values from -6 to 6
- down_weight: bfloat16 [7168, 4096], P('narrow'), may hold values from -0.0625 to 0.0625
Outputs:
- head_grad: bfloat16 [1024, 4096], P('wide', 'narrow')
- gate_grad: bfloat16 [1024, 7168], P('wide', 'narrow')
- up_grad: bfloat16 [1024, 7168], P('wide', 'narrow')
Inputs may be any that keep to these rules, and one draw needn't show every extreme that they name: The first block_counts[b, s] entries of block_tiles[b, s] are distinct; the other entries are ignored. `block_counts`: some row block has 4 active tiles in some shard; one shard has exactly 16 active tiles over all row blocks, and no shard has more.
All inputs are finite; a program needn't handle non-finite values.
Results may differ from a plain program's by a relative error of at most 0.0035.
The roundings to bfloat16 on the way count: a program that leaves them out, or rounds other values in their place, can miss the bound.
Values may be sent and summed in bfloat16 or wider, within the bound.
No kernel may reach another device: no remote copies, remote signals or barrier semaphores. Data moves between devices by JAX's collectives and lax.ppermute only.
A program may use at most 128 MiB of HBM per device.

v0:
```python
import jax
import jax.numpy as jnp
from jax import lax
from jax.sharding import PartitionSpec as P

TILE = 128


def slot_table(tiles_here, counts_here, slot_count):
    block_total, per_block = tiles_here.shape
    slot_live = (jnp.arange(per_block, dtype=jnp.int32)[None, :] < counts_here[:, None]).reshape(-1)
    position = jnp.cumsum(slot_live.astype(jnp.int32)) - 1
    select = (position[None, :] == jnp.arange(slot_count, dtype=jnp.int32)[:, None]) & slot_live[
        None, :
    ]
    chosen = select.astype(jnp.int32)
    block_ids = jnp.repeat(jnp.arange(block_total, dtype=jnp.int32), per_block)
    slot_blocks = jnp.sum(chosen * block_ids[None, :], axis=1)
    slot_tiles = jnp.sum(chosen * tiles_here.reshape(-1)[None, :], axis=1)
    return (slot_blocks, slot_tiles, jnp.sum(chosen, axis=1) > 0)


def cell_weights(logits, lse_rows, scale_rows, slot_live):
    scaled = jnp.exp(logits - lse_rows[:, :, None]) * scale_rows[:, :, None]
    return jnp.where(slot_live[:, None, None], scaled, 0.0).astype(jnp.bfloat16)


def on_device(
    hidden,
    head_weight,
    lse,
    targets,
    loss_weight,
    block_tiles,
    block_counts,
    gate_pre,
    up_pre,
    down_weight,
):
    features = hidden.shape[1]
    row_count = hidden.shape[0]
    vocab_here = head_weight.shape[0]
    offset = lax.axis_index("wide") * vocab_here
    gathered = lax.all_gather(hidden, "wide", axis=0, tiled=True)
    blocks = gathered.shape[0] // TILE
    weight_tiles = head_weight.reshape(vocab_here // TILE, TILE, features)
    tiles_here = block_tiles[:, 0, :]
    counts_here = block_counts[:, 0]
    per_block = tiles_here.shape[1]
    lse_blocks = lse.reshape(blocks, TILE)
    scale_blocks = loss_weight.reshape(blocks, TILE)
    slot_count = blocks // 2 * per_block
    slot_blocks, slot_tiles, slot_live = slot_table(tiles_here, counts_here, slot_count)
    picked = jnp.take(weight_tiles, slot_tiles, axis=0)
    row_blocks = jnp.take(gathered.reshape(blocks, TILE, features), slot_blocks, axis=0)
    partial_value = jnp.einsum(
        "srd,scd->src", row_blocks, picked, preferred_element_type=jnp.float32
    )
    slot_lse = jnp.take(lse_blocks, slot_blocks, axis=0)
    slot_scale = jnp.take(scale_blocks, slot_blocks, axis=0)
    logits = lax.psum(partial_value, "narrow")
    cell_probs = cell_weights(logits, slot_lse, slot_scale, slot_live)
    contrib = jnp.einsum("src,scd->srd", cell_probs, picked, preferred_element_type=jnp.float32)
    contrib = contrib.reshape(slot_count, TILE * features)
    block_span = row_count * lax.axis_size("wide") // TILE
    wanted = jnp.arange(block_span, dtype=jnp.int32)
    member = ((slot_blocks[None, :] == wanted[:, None]) & slot_live[None, :]).astype(jnp.float32)
    softmax_part = jnp.dot(
        member, contrib, precision=lax.Precision.HIGHEST, preferred_element_type=jnp.float32
    ).reshape(row_count * lax.axis_size("wide"), features)
    local_ids = targets - offset
    inside = (local_ids >= 0) & (local_ids < vocab_here)
    target_rows = jnp.take(head_weight, jnp.clip(local_ids, 0, vocab_here - 1), axis=0).astype(
        jnp.float32
    )
    factor = jnp.where(inside, loss_weight, 0.0)
    head_grad = lax.psum_scatter(
        softmax_part - factor[:, None] * target_rows, "wide", scatter_dimension=0, tiled=True
    ).astype(jnp.bfloat16)
    unit_grad = lax.dot_general(
        lax.all_gather(head_grad, "narrow", axis=1, tiled=True),
        down_weight,
        (((1,), (1,)), ((), ())),
        preferred_element_type=jnp.float32,
    )
    gate_value = gate_pre.astype(jnp.float32)
    up_value = up_pre.astype(jnp.float32)
    gate_sig = jax.nn.sigmoid(gate_value)
    up_grad = (unit_grad * gate_value * gate_sig).astype(jnp.bfloat16)
    gate_grad = (unit_grad * up_value * gate_sig * (1.0 + gate_value * (1.0 - gate_sig))).astype(
        jnp.bfloat16
    )
    return (head_grad, gate_grad, up_grad)


def solution(mesh):
    in_specs = (
        P("wide", "narrow"),
        P("wide", "narrow"),
        P(),
        P(),
        P(),
        P(None, "wide", None),
        P(None, "wide"),
        P("wide", "narrow"),
        P("wide", "narrow"),
        P("narrow", None),
    )
    out_specs = (P("wide", "narrow"), P("wide", "narrow"), P("wide", "narrow"))
    return jax.shard_map(
        on_device, mesh=mesh, in_specs=in_specs, out_specs=out_specs, check_vma=False
    )
```

profile of v0, /device:TPU:0, one launch (start us, length us, event | category | flops | bytes accessed | tf_op | source)
XLA Modules:
  0.0 223.7 jit_solution(11905009591479860913)
XLA Ops:
  7.2 0.7 all-gather.3.cloned.1.call-update
  8.0 0.7 iota_compare_fusion.2
  8.9 0.8 copy.18
  9.8 0.1 add_reduce_fusion
  10.0 0.2 convert_reduce_fusion
  10.1 0.6 gather_fusion.3
  10.7 1.2 gather_fusion.4
  12.0 6.1 %gather_fusion.1 = bf16[16,128,1024]{2,1,0:T(8,128)(2,1)} fusion(bf16[32,128,1024]{2,1,0:T(8,128)(2,1)} %bitcast.21, s32[1024]{0:T(1024)S(1)} %pad_clamp_fusion.1), kind=kCustom, calls=%fused_computation.3 | custom fusion | bytes 8388672 | tf_op jit(solution)/shard_map/jit(_take)/gather | solution.py:54
  18.1 22.3 %all-gather.3.cloned.1.call-done = bf16[1024,1024]{1,0:T(8,128)(2,1)} async-done(((bf16[128,1024]{1,0:T(8,128)(2,1)}), bf16[1024,1024]{1,0:T(8,128)(2,1)}) %all-gather.3.cloned.1.call-update) | async-done | bytes 2097168 | tf_op jit(solution)/shard_map/all_gather | solution.py:44
  40.4 4.4 %gather_fusion = bf16[16,128,1024]{2,1,0:T(8,128)(2,1)} fusion(bf16[8,128,1024]{2,1,0:T(8,128)(2,1)} %bitcast.24, s32[1024]{0:T(1024)S(1)} %pad_clamp_fusion.2), kind=kCustom, calls=%fused_computation.2 | custom fusion | bytes 8388672 | tf_op jit(solution)/shard_map/jit(_take)/gather | solution.py:55
  44.8 6.0 %fusion = f32[16,128,128]{2,1,0:T(8,128)} fusion(bf16[16,128,1024]{2,1,0:T(8,128)(2,1)} %gather_fusion, pred[16]{0:T(512)(128)(4,1)S(1)} %get-tuple-element.14, bf16[16,128,1024]{2,1,0:T(8,128)(2,1)} %gather_fusion.1, pred[16]{0:T(512)(128)(4,1)S(1)} %get-tuple-element.13), kind=kOutput, calls=%fused_computation.6 | convolution fusion | flops 541065216 | bytes 9437216 | tf_op jit(solution)/shard_map/srd,scd->src/dot_general | solution.py:56
  50.8 0.2 reduce-scatter.2.cloned.1.call-start
  51.1 9.4 %gather_fusion.2 = bf16[1024,1024]{1,0:T(8,128)(2,1)S(1)} fusion(bf16[4096,1024]{1,0:T(8,128)(2,1)} %param.13, s32[1024]{0:T(1024)S(1)} %fusion.21), kind=kCustom, calls=%fused_computation.4 | custom fusion | bytes 4198400 | tf_op jit(solution)/shard_map/jit(_take)/gather | solution.py:73
  60.7 42.2 %all-reduce.2.cloned.1.call-done = f32[16,128,128]{2,1,0:T(8,128)} async-done(((f32[16,128,128]{2,1,0:T(8,128)}), f32[16,128,128]{2,1,0:T(8,128)}) %all-reduce.2.cloned.1.call-update) | async-done | bytes 1048592 | tf_op jit(solution)/shard_map/psum | solution.py:61
  102.9 3.8 %fusion.4 = f32[16,128,1024]{2,1,0:T(8,128)S(1)} fusion(bf16[16,128,1024]{2,1,0:T(8,128)(2,1)} %gather_fusion.1, pred[16]{0:T(512)(128)(4,1)S(1)} %get-tuple-element.13, f32[16,128,128]{2,1,0:T(8,128)} %all-reduce.2.cloned.1.call-done, f32[16,128]{1,0:T(8,128)S(1)} %get-tuple-element.10, f32[16,128]{1,0:T(8,128)S(1)} %get-tuple-element.9, ...), kind=kOutput, calls=%fused_computation.11 | convolution fusion | flops 540016640 | bytes 13647904 | tf_op jit(solution)/shard_map/src,scd->srd/dot_general | solution.py:63
  106.7 4.9 %copy.19 = f32[2,8,128,1024]{3,1,2,0:T(8,128)S(1)} copy(f32[2,8,128,1024]{3,2,1,0:T(8,128)S(1)} %bitcast.22) | data formatting | bytes 16777216
  111.6 4.4 %fusion.19 = f32[8,131072]{1,0:T(8,128)} fusion(f32[16,131072]{1,0:T(8,128)S(1)} %bitcast.23, s32[16]{0:T(128)S(1)} %get-tuple-element.6, pred[16]{0:T(512)(128)(4,1)S(1)} %broadcast_compare_fusion), kind=kOutput, calls=%fused_computation.43 | convolution fusion | flops 201326848 | bytes 12582992 | tf_op jit(solution)/shard_map/dot_general | solution.py:68
  116.0 4.9 %reshape.152 = f32[1024,1024]{1,0:T(8,128)} reshape(f32[8,131072]{1,0:T(8,128)} %fusion.19) | data formatting | bytes 8388608 | tf_op jit(solution)/shard_map/reshape | solution.py:70
  120.9 4.1 %multiply_subtract_fusion = f32[1024,1024]{1,0:T(8,128)} fusion(f32[1024,1024]{1,0:T(8,128)} %reshape.152, bf16[1024,1024]{1,0:T(8,128)(2,1)S(1)} %gather_fusion.2, f32[1024]{0:T(1024)S(1)} %and_select_fusion, pred[1024]{0:T(1024)(128)(4,1)S(1)} %compare_and_fusion), kind=kLoop, calls=%fused_computation.5 | loop fusion | flops 4194304 | bytes 10490880 | tf_op jit(solution)/shard_map/sub | solution.py:78
  125.0 0.3 all-gather.5.cloned.1.call-start
  125.3 50.3 %reduce-scatter.2.cloned.1.call-done = f32[128,1024]{1,0:T(8,128)} async-done(((f32[1024,1024]{1,0:T(8,128)}), f32[128,1024]{1,0:T(8,128)}) %reduce-scatter.2.cloned.1.call-update) | async-done | bytes 524304 | tf_op jit(solution)/shard_map/reduce_scatter | solution.py:77
  175.6 1.8 convert_element_type.45
  177.4 28.2 %all-gather.5.cloned.1.call-done = bf16[128,4096]{1,0:T(8,128)(2,1)} async-done(((bf16[128,1024]{1,0:T(8,128)(2,1)}), bf16[128,4096]{1,0:T(8,128)(2,1)}) %all-gather.5.cloned.1.call-update) | async-done | bytes 1048592 | tf_op jit(solution)/shard_map/all_gather | solution.py:81
  205.6 11.5 %fusion.12 = (bf16[128,1792]{1,0:T(8,128)(2,1)}, bf16[128,1792]{1,0:T(8,128)(2,1)}) fusion(bf16[128,1792]{1,0:T(8,128)(2,1)S(1)} %copy-done.4, bf16[128,1792]{1,0:T(8,128)(2,1)S(1)} %copy-done.5, bf16[128,4096]{1,0:T(8,128)(2,1)} %all-gather.5.cloned.1.call-done, bf16[1792,4096]{1,0:T(8,128)(2,1)} %param.21), kind=kOutput, calls=%fused_computation.23 | convolution fusion | flops 1882488832 | bytes 17563648 | tf_op jit(solution)/shard_map/dot_general | solution.py:80
  (35 shorter events, 0.7 us)
Async XLA Ops:
  7.2 3.0 %copy-start = (f32[1024]{0:T(1024)S(1)}, f32[1024]{0:T(1024)}, u32[]{:S(2)}) copy-start(f32[1024]{0:T(1024)} %param.14) | copy-start | bytes 12292
  7.2 33.2 %all-gather.3.cloned.1.call-start = ((), (), s32[]{:S(2)}) async-start(), calls=%async_computation.1 | async-start | bytes 2359296 | tf_op jit(solution)/shard_map/all_gather | solution.py:44
  7.9 95.0 %all-reduce.2.cloned.1.call-start = ((), (), s32[]{:S(2)}) async-start(), calls=%async_computation.2 | async-start | bytes 2097152 | tf_op jit(solution)/shard_map/psum | solution.py:61
  44.8 6.3 %copy-start.3 = (s32[1024]{0:T(1024)S(1)}, s32[1024]{0:T(1024)}, u32[]{:S(2)}) copy-start(s32[1024]{0:T(1024)} %param.15) | copy-start | bytes 12292
  50.8 124.7 %reduce-scatter.2.cloned.1.call-start = ((), (), s32[]{:S(2)}) async-start(), calls=%async_computation.3 | async-start | bytes 4718592 | tf_op jit(solution)/shard_map/reduce_scatter | solution.py:77
  51.1 9.5 %copy-start.2 = (f32[1024]{0:T(1024)S(1)}, f32[1024]{0:T(1024)}, u32[]{:S(2)}) copy-start(f32[1024]{0:T(1024)} %param.16) | copy-start | bytes 12292
  125.0 80.6 %copy-start.4 = (bf16[128,1792]{1,0:T(8,128)(2,1)S(1)}, bf16[128,1792]{1,0:T(8,128)(2,1)}, u32[]{:S(2)}) copy-start(bf16[128,1792]{1,0:T(8,128)(2,1)} %param.19) | copy-start | bytes 1376260
  125.0 80.6 %copy-start.5 = (bf16[128,1792]{1,0:T(8,128)(2,1)S(1)}, bf16[128,1792]{1,0:T(8,128)(2,1)}, u32[]{:S(2)}) copy-start(bf16[128,1792]{1,0:T(8,128)(2,1)} %param.20) | copy-start | bytes 1376260
  125.0 80.6 %all-gather.5.cloned.1.call-start = ((), (), s32[]{:S(2)}) async-start(), calls=%async_computation.4 | async-start | bytes 1310720 | tf_op jit(solution)/shard_map/all_gather | solution.py:81
  205.6 11.5 %copy-start.1 = (f32[1024]{0:T(1024)S(1)}, f32[1024]{0:T(1024)}, u32[]{:S(2)}) copy-start(f32[1024]{0:T(1024)} %param.14) | copy-start | bytes 12292
Sparse Core Ops, SparseCore 0:
  9.9 30.4 all-gather.2
  50.9 51.8 all-reduce.1
  125.1 50.4 reduce-scatter.1
  177.6 27.9 all-gather.4
where the time goes:
time: 224 us
  waiting for transfers between devices  144 us (64%)
  local copies, waits for them, and re-layouts  32.6 us (15%)
  matrix products  25.8 us (12%)
  between operations  13.9 us (6%)
  other arithmetic  7.04 us (3%)
    reduce_scatter x1, waiting for transfers between devices, on_device(): lax.psum_scatter(softmax_part - factor[:, None] * target_rows, 'wide', sc...  50.3 us
    psum x1, waiting for transfers between devices, on_device(): logits = lax.psum(partial_value, 'narrow')  42.2 us
    all_gather x1, waiting for transfers between devices, on_device(): lax.all_gather(head_grad, 'narrow', axis=1, tiled=True)  28.2 us
    all_gather x1, waiting for transfers between devices, on_device(): gathered = lax.all_gather(hidden, 'wide', axis=0, tiled=True)  22.3 us
    dot_general x1, matrix products, on_device(): lax.dot_general(lax.all_gather(head_grad, 'narrow', axis=1, tiled=True),...  11.5 us
    gather x1, local copies, waits for them, and re-layouts, on_device(): jnp.take(head_weight, jnp.clip(local_ids, 0, vocab_here - 1), axis=0)  9.44 us
    gather x1, local copies, waits for them, and re-layouts, on_device(): picked = jnp.take(weight_tiles, slot_tiles, axis=0)  6.13 us
    dot_general x1, matrix products, on_device(): jnp.einsum('srd,scd->src', row_blocks, picked, preferred_element_type=jnp...  6 us
  transfers between devices with their start and end apart: 4, of which 4 were waited for; matrix products, arithmetic and copies ran while one was open for 9% of the time, Pallas kernels for 0%

commit v1 on v0

--- a/solution.py
+++ b/solution.py
@@ -58,7 +58,7 @@
     )
     slot_lse = jnp.take(lse_blocks, slot_blocks, axis=0)
     slot_scale = jnp.take(scale_blocks, slot_blocks, axis=0)
-    logits = lax.psum(partial_value, "narrow")
+    logits = jnp.sum(lax.all_gather(partial_value, "narrow"), axis=0)
     cell_probs = cell_weights(logits, slot_lse, slot_scale, slot_live)
     contrib = jnp.einsum("src,scd->srd", cell_probs, picked, preferred_element_type=jnp.float32)
     contrib = contrib.reshape(slot_count, TILE * features)

time: 224 us -> 254 us (1.13)
  waiting for transfers between devices: 144 us -> 172 us
  other arithmetic: 7.04 us -> 9.67 us
    all_gather x0 -> x1, waiting for transfers between devices: none -> 69.9 us  [on_device(): logits = jnp.sum(lax.all_gather(partial_value, 'narrow'), axis=0)]
    psum x1 -> x0, waiting for transfers between devices: 42.2 us -> none  [on_device(): logits = lax.psum(partial_value, 'narrow')]
    reduce_sum x0 -> x1, other arithmetic: none -> 2.64 us  [on_device(): logits = jnp.sum(lax.all_gather(partial_value, 'narrow'), axis=0)]
  transfers between devices with their start and end apart: 4 -> 4, of which waited for: 4 -> 4; matrix products, arithmetic and copies ran while one was open for 9% -> 7% of each run, Pallas kernels for 0% -> 0%
where the time goes in v1:
time: 254 us
  waiting for transfers between devices  172 us (68%)
  local copies, waits for them, and re-layouts  32 us (13%)
  matrix products  25.2 us (10%)
  between operations  13.9 us (5%)
  other arithmetic  9.67 us (4%)
    all_gather x1, waiting for transfers between devices, on_device(): logits = jnp.sum(lax.all_gather(partial_value, 'narrow'), axis=0)  69.9 us
    reduce_scatter x1, waiting for transfers between devices, on_device(): lax.psum_scatter(softmax_part - factor[:, None] * target_rows, 'wide', sc...  49.5 us
    all_gather x1, waiting for transfers between devices, on_device(): lax.all_gather(head_grad, 'narrow', axis=1, tiled=True)  28.2 us
    all_gather x1, waiting for transfers between devices, on_device(): gathered = lax.all_gather(hidden, 'wide', axis=0, tiled=True)  24.1 us
    dot_general x1, matrix products, on_device(): lax.dot_general(lax.all_gather(head_grad, 'narrow', axis=1, tiled=True),...  11.5 us
    gather x1, local copies, waits for them, and re-layouts, on_device(): jnp.take(head_weight, jnp.clip(local_ids, 0, vocab_here - 1), axis=0)  9.44 us
    gather x1, local copies, waits for them, and re-layouts, on_device(): picked = jnp.take(weight_tiles, slot_tiles, axis=0)  6.13 us
    dot_general x1, matrix products, on_device(): jnp.einsum('srd,scd->src', row_blocks, picked, preferred_element_type=jnp...  6.01 us
  transfers between devices with their start and end apart: 4, of which 4 were waited for; matrix products, arithmetic and copies ran while one was open for 7% of the time, Pallas kernels for 0%

profile of v1, /device:TPU:0, one launch (start us, length us, event | category | flops | bytes accessed | tf_op | source)
XLA Modules:
  0.0 253.7 jit_solution(13107658467184058478)
XLA Ops:
  7.2 0.7 all-gather.5.cloned.1.call-update
  8.0 0.7 iota_compare_fusion.2
  8.9 0.8 copy.20
  9.9 0.2 convert_reduce_fusion
  10.1 6.1 %gather_fusion.1 = bf16[16,128,1024]{2,1,0:T(8,128)(2,1)} fusion(bf16[32,128,1024]{2,1,0:T(8,128)(2,1)} %bitcast.22, s32[1024]{0:T(1024)S(1)} %pad_clamp_fusion.1), kind=kCustom, calls=%fused_computation.3 | custom fusion | bytes 8388672 | tf_op jit(solution)/shard_map/jit(_take)/gather | solution.py:54
  16.3 24.1 %all-gather.5.cloned.1.call-done = bf16[1024,1024]{1,0:T(8,128)(2,1)} async-done(((bf16[128,1024]{1,0:T(8,128)(2,1)}), bf16[1024,1024]{1,0:T(8,128)(2,1)}) %all-gather.5.cloned.1.call-update) | async-done | bytes 2097168 | tf_op jit(solution)/shard_map/all_gather | solution.py:44
  40.4 4.4 %gather_fusion = bf16[16,128,1024]{2,1,0:T(8,128)(2,1)} fusion(bf16[8,128,1024]{2,1,0:T(8,128)(2,1)} %bitcast.25, s32[1024]{0:T(1024)S(1)} %pad_clamp_fusion.2), kind=kCustom, calls=%fused_computation.2 | custom fusion | bytes 8388672 | tf_op jit(solution)/shard_map/jit(_take)/gather | solution.py:55
  44.8 6.0 %fusion = f32[16,128,128]{2,1,0:T(8,128)} fusion(bf16[16,128,1024]{2,1,0:T(8,128)(2,1)} %gather_fusion, pred[16]{0:T(512)(128)(4,1)S(1)} %get-tuple-element.14, bf16[16,128,1024]{2,1,0:T(8,128)(2,1)} %gather_fusion.1, pred[16]{0:T(512)(128)(4,1)S(1)} %get-tuple-element.13), kind=kOutput, calls=%fused_computation.6 | convolution fusion | flops 541065216 | bytes 9437216 | tf_op jit(solution)/shard_map/srd,scd->src/dot_general | solution.py:56
  50.8 0.2 reduce-scatter.2.cloned.1.call-start
  51.1 0.6 gather_fusion.3
  51.7 0.6 gather_fusion.4
  52.3 9.4 %gather_fusion.2 = bf16[1024,1024]{1,0:T(8,128)(2,1)S(1)} fusion(bf16[4096,1024]{1,0:T(8,128)(2,1)} %param.13, s32[1024]{0:T(1024)S(1)} %fusion.21), kind=kCustom, calls=%fused_computation.4 | custom fusion | bytes 4198400 | tf_op jit(solution)/shard_map/jit(_take)/gather | solution.py:73
  61.8 69.9 %all-gather.9.cloned.1.call-done = f32[64,128,128]{2,1,0:T(8,128)} async-done(((f32[16,128,128]{2,1,0:T(8,128)}), f32[64,128,128]{2,1,0:T(8,128)}) %all-gather.9.cloned.1.call-update) | async-done | bytes 4194320 | tf_op jit(solution)/shard_map/all_gather | solution.py:61
  131.7 2.6 %reduce_sum.45 = f32[16,128,128]{2,1,0:T(8,128)S(1)} reduce(f32[4,16,128,128]{3,2,1,0:T(8,128)} %bitcast.26, f32[]{:T(128)} %constant.72.clone.1), dimensions={0}, to_apply=%region_4.5 | reduce | flops 786432 | bytes 5242884 | tf_op jit(solution)/shard_map/reduce_sum | solution.py:61
  134.4 3.2 %fusion.4 = f32[16,128,1024]{2,1,0:T(8,128)S(1)} fusion(bf16[16,128,1024]{2,1,0:T(8,128)(2,1)} %gather_fusion.1, pred[16]{0:T(512)(128)(4,1)S(1)} %get-tuple-element.13, f32[16,128,128]{2,1,0:T(8,128)S(1)} %reduce_sum.45, f32[16,128]{1,0:T(8,128)S(1)} %get-tuple-element.10, f32[16,128]{1,0:T(8,128)S(1)} %get-tuple-element.9, ...), kind=kOutput, calls=%fused_computation.11 | convolution fusion | flops 540016640 | bytes 13647904 | tf_op jit(solution)/shard_map/src,scd->srd/dot_general | solution.py:63
  137.6 4.9 %copy.21 = f32[2,8,128,1024]{3,1,2,0:T(8,128)S(1)} copy(f32[2,8,128,1024]{3,2,1,0:T(8,128)S(1)} %bitcast.23) | data formatting | bytes 16777216
  142.4 4.4 %fusion.19 = f32[8,131072]{1,0:T(8,128)} fusion(f32[16,131072]{1,0:T(8,128)S(1)} %bitcast.24, s32[16]{0:T(128)S(1)} %get-tuple-element.6, pred[16]{0:T(512)(128)(4,1)S(1)} %broadcast_compare_fusion), kind=kOutput, calls=%fused_computation.43 | convolution fusion | flops 201326848 | bytes 12582992 | tf_op jit(solution)/shard_map/dot_general | solution.py:68
  146.9 4.9 %reshape.152 = f32[1024,1024]{1,0:T(8,128)} reshape(f32[8,131072]{1,0:T(8,128)} %fusion.19) | data formatting | bytes 8388608 | tf_op jit(solution)/shard_map/reshape | solution.py:70
  151.8 4.1 %multiply_subtract_fusion = f32[1024,1024]{1,0:T(8,128)} fusion(f32[1024,1024]{1,0:T(8,128)} %reshape.152, bf16[1024,1024]{1,0:T(8,128)(2,1)S(1)} %gather_fusion.2, f32[1024]{0:T(1024)S(1)} %and_select_fusion, pred[1024]{0:T(1024)(128)(4,1)S(1)} %compare_and_fusion), kind=kLoop, calls=%fused_computation.5 | loop fusion | flops 4194304 | bytes 10490880 | tf_op jit(solution)/shard_map/sub | solution.py:78
  155.9 0.3 all-gather.7.cloned.1.call-start
  156.1 49.5 %reduce-scatter.2.cloned.1.call-done = f32[128,1024]{1,0:T(8,128)} async-done(((f32[1024,1024]{1,0:T(8,128)}), f32[128,1024]{1,0:T(8,128)}) %reduce-scatter.2.cloned.1.call-update) | async-done | bytes 524304 | tf_op jit(solution)/shard_map/reduce_scatter | solution.py:77
  205.7 1.8 convert_element_type.45
  207.5 28.2 %all-gather.7.cloned.1.call-done = bf16[128,4096]{1,0:T(8,128)(2,1)} async-done(((bf16[128,1024]{1,0:T(8,128)(2,1)}), bf16[128,4096]{1,0:T(8,128)(2,1)}) %all-gather.7.cloned.1.call-update) | async-done | bytes 1048592 | tf_op jit(solution)/shard_map/all_gather | solution.py:81
  235.7 11.5 %fusion.12 = (bf16[128,1792]{1,0:T(8,128)(2,1)}, bf16[128,1792]{1,0:T(8,128)(2,1)}) fusion(bf16[128,1792]{1,0:T(8,128)(2,1)S(1)} %copy-done.4, bf16[128,1792]{1,0:T(8,128)(2,1)S(1)} %copy-done.5, bf16[128,4096]{1,0:T(8,128)(2,1)} %all-gather.7.cloned.1.call-done, bf16[1792,4096]{1,0:T(8,128)(2,1)} %param.21), kind=kOutput, calls=%fused_computation.23 | convolution fusion | flops 1882488832 | bytes 17563648 | tf_op jit(solution)/shard_map/dot_general | solution.py:80
  (36 shorter events, 0.8 us)
Async XLA Ops:
  7.2 43.9 %copy-start = (f32[1024]{0:T(1024)S(1)}, f32[1024]{0:T(1024)}, u32[]{:S(2)}) copy-start(f32[1024]{0:T(1024)} %param.14) | copy-start | bytes 12292
  7.2 33.2 %all-gather.5.cloned.1.call-start = ((), (), s32[]{:S(2)}) async-start(), calls=%async_computation.1 | async-start | bytes 2359296 | tf_op jit(solution)/shard_map/all_gather | solution.py:44
  7.9 123.8 %all-gather.9.cloned.1.call-start = ((), (), s32[]{:S(2)}) async-start(), calls=%async_computation.4 | async-start | bytes 5242880 | tf_op jit(solution)/shard_map/all_gather | solution.py:61
  44.8 6.9 %copy-start.2 = (f32[1024]{0:T(1024)S(1)}, f32[1024]{0:T(1024)}, u32[]{:S(2)}) copy-start(f32[1024]{0:T(1024)} %param.16) | copy-start | bytes 12292
  44.8 7.5 %copy-start.3 = (s32[1024]{0:T(1024)S(1)}, s32[1024]{0:T(1024)}, u32[]{:S(2)}) copy-start(s32[1024]{0:T(1024)} %param.15) | copy-start | bytes 12292
  50.8 154.8 %reduce-scatter.2.cloned.1.call-start = ((), (), s32[]{:S(2)}) async-start(), calls=%async_computation.2 | async-start | bytes 4718592 | tf_op jit(solution)/shard_map/reduce_scatter | solution.py:77
  155.8 79.8 %copy-start.4 = (bf16[128,1792]{1,0:T(8,128)(2,1)S(1)}, bf16[128,1792]{1,0:T(8,128)(2,1)}, u32[]{:S(2)}) copy-start(bf16[128,1792]{1,0:T(8,128)(2,1)} %param.19) | copy-start | bytes 1376260
  155.8 79.8 %copy-start.5 = (bf16[128,1792]{1,0:T(8,128)(2,1)S(1)}, bf16[128,1792]{1,0:T(8,128)(2,1)}, u32[]{:S(2)}) copy-start(bf16[128,1792]{1,0:T(8,128)(2,1)} %param.20) | copy-start | bytes 1376260
  155.9 79.8 %all-gather.7.cloned.1.call-start = ((), (), s32[]{:S(2)}) async-start(), calls=%async_computation.3 | async-start | bytes 1310720 | tf_op jit(solution)/shard_map/all_gather | solution.py:81
  235.7 11.5 %copy-start.1 = (f32[1024]{0:T(1024)S(1)}, f32[1024]{0:T(1024)}, u32[]{:S(2)}) copy-start(f32[1024]{0:T(1024)} %param.14) | copy-start | bytes 12292
Sparse Core Ops, SparseCore 0:
  9.9 30.4 all-gather.4
  51.0 80.7 all-gather.8
  156.0 49.6 reduce-scatter.1
  207.7 27.9 all-gather.6
